TPU v7x, 128 devices: a whole 4x4x4 slice. The times are simulated.
128 devices in a mesh: lat: 16 (over x, z), dep: 8 (over y, core).
Axes of the slice: x: 4, y: 4, z: 4, core: 2. Of those that a mesh axis runs over, the one named last changes fastest.
Arguments:
- state: float32 [64, 64, 128], P('lat', 'dep'), may hold values from 0.2 to 1
- kappa: float32 [64, 64, 128], P('lat', 'dep'), may hold values from 0.3 to 3
- rate: float32 [64, 64], P('lat', 'dep'), may hold values from 1 to 4
- grads: float32 [3, 64, 64], replicated, may hold values from -0.75 to 0.75
- lift: float32 [4, 32, 128], replicated, may hold values from -0.375 to 0.375
- rhs: float32 [64, 64, 32, 128], P('lat', 'dep'), may hold values from -18 to 18
Outputs:
- update: float32 [64, 64, 32, 128], P('lat', 'dep')
All inputs are finite; a program needn't handle non-finite values.
Results may differ from a plain program's by a relative error of at most 0.0003.
Values sent between devices are 32-bit elements; how exact they have to be, the bound alone decides.
A program may use at most 128 MiB of HBM per device.

v0:
```python
import jax
import jax.numpy as jnp
from jax import lax
from jax.sharding import PartitionSpec as P

KRY = 8
highest = lax.Precision.HIGHEST
mass_shift = 0.25


def with_halo(cells, sides, width, closed):
    for axis, dim in sides:
        count = lax.axis_size(axis)
        ends = count if closed else count - 1
        head = lax.slice_in_dim(cells, 0, width, axis=dim)
        tail = lax.slice_in_dim(cells, cells.shape[dim] - width, cells.shape[dim], axis=dim)
        cells = jnp.concatenate(
            [
                lax.ppermute(tail, axis, [(i, (i + 1) % count) for i in range(ends)]),
                cells,
                lax.ppermute(head, axis, [((i + 1) % count, i) for i in range(ends)]),
            ],
            axis=dim,
        )
    return cells


def from_behind(value, axis, steps):
    count = lax.axis_size(axis)
    pairs = [(source, (source + steps) % count) for source in range(count)]
    return lax.ppermute(value, axis, pairs)


def passed_along(array, axis, by):
    peers = lax.axis_size(axis)
    pairs = [(i, i + by) for i in range(peers) if 0 <= i + by < peers]
    return lax.ppermute(array, axis, pairs)


def face_table():
    unknown = jnp.arange(128, dtype=jnp.int32)[:, None]
    column = jnp.arange(128, dtype=jnp.int32)[None, :]
    face_id = column // 32
    species = column // 16 % 2
    along_one = column % 16 // 4
    along_two = column % 4
    edge_pos = 3 * (face_id % 2)
    is_lateral = face_id < 2
    node_x = jnp.where(is_lateral, edge_pos, along_one)
    node_y = jnp.where(is_lateral, along_one, along_two)
    node_z = jnp.where(is_lateral, along_two, edge_pos)
    target = species * 64 + node_x * 16 + node_y * 4 + node_z
    return (unknown == target).astype(jnp.float32)


def pairing_table():
    unknown = jnp.arange(128, dtype=jnp.int32)
    return (unknown[:, None] % 64 == unknown[None, :] % 64).astype(jnp.float32)


def element_tiles(kappa_rows, state_rows, rate_rows, grads, select):
    row_count = kappa_rows.shape[0]
    split_kappa = kappa_rows.reshape(row_count, 2, 64)
    stiffness = jnp.einsum("dqi,nsq,dqj->nsij", grads, split_kappa, grads, precision=highest)
    zero_block = jnp.zeros((row_count, 64, 64), jnp.float32)
    top_half = jnp.concatenate([stiffness[:, 0], zero_block], axis=2)
    bottom_half = jnp.concatenate([zero_block, stiffness[:, 1]], axis=2)
    face_kappa = jnp.dot(kappa_rows, select, precision=highest)
    penalty = jnp.dot(face_kappa, select.T, precision=highest)
    partner = jnp.concatenate([state_rows[:, 64:], state_rows[:, :64]], axis=1)
    identity = jnp.eye(128, dtype=jnp.float32)
    diag_tiles = jnp.concatenate([top_half, bottom_half], axis=1)
    diag_tiles = diag_tiles + identity[None] * (mass_shift + penalty)[:, None, :]
    diag_tiles = diag_tiles + pairing_table()[None] * (rate_rows[:, None] * partner)[:, None, :]
    return (diag_tiles, face_kappa)


def apply_operator(vectors, diag_tiles, couple, select):
    lat_rows = vectors.shape[0]
    dep_rows = vectors.shape[1]
    columns = vectors.shape[2]
    traces = jnp.einsum("aevu,uk->aevk", vectors, select, precision=highest)
    lat_rims = jnp.stack([traces[0, :, :, 0:32], traces[-1, :, :, 32:64]]).reshape(
        2, dep_rows, columns * 32
    )
    lat_wide = with_halo(lat_rims, (("lat", 0),), 1, True)
    prev_lat = lat_wide[0].reshape(dep_rows, columns, 32)
    next_lat = lat_wide[3].reshape(dep_rows, columns, 32)
    dep_rims = jnp.stack([traces[:, 0, :, 64:96], traces[:, -1, :, 96:128]]).reshape(
        2, lat_rows, columns * 32
    )
    dep_wide = with_halo(dep_rims, (("dep", 0),), 1, False)
    prev_dep = dep_wide[0].reshape(lat_rows, columns, 32)
    next_dep = dep_wide[3].reshape(lat_rows, columns, 32)
    from_left = jnp.concatenate([prev_lat[None], traces[:-1, :, :, 32:64]], axis=0)
    from_right = jnp.concatenate([traces[1:, :, :, 0:32], next_lat[None]], axis=0)
    from_below = jnp.concatenate([prev_dep[:, None], traces[:, :-1, :, 96:128]], axis=1)
    from_above = jnp.concatenate([traces[:, 1:, :, 64:96], next_dep[:, None]], axis=1)
    near_traces = jnp.concatenate([from_left, from_right, from_below, from_above], axis=-1)
    own_part = jnp.einsum("aeij,aevj->aevi", diag_tiles, vectors, precision=highest)
    coupled = jnp.einsum("aeki,aevk->aevi", couple, near_traces, precision=highest)
    return own_part - coupled


def inner_local(left_block, right_block):
    return jnp.einsum("aevu,aewu->vw", left_block, right_block, precision=highest)


def combine_columns(vectors, matrix):
    return jnp.einsum("aevu,vw->aewu", vectors, matrix, precision=highest)


def factor(gram_matrix):
    lower_factor = jnp.linalg.cholesky(gram_matrix)
    identity = jnp.eye(gram_matrix.shape[0], dtype=gram_matrix.dtype)
    inverse = jax.scipy.linalg.solve_triangular(lower_factor, identity, lower=True)
    return (lower_factor.T, inverse.T)


def per_device(state, kappa, rate, grads, lift, rhs):
    select = face_table()

    def one_row(row_data):
        return element_tiles(row_data[0], row_data[1], row_data[2], grads, select)

    diag_tiles, face_kappa = lax.map(one_row, (kappa, state, rate))
    lat_end = face_kappa[-1, :, 32:64]
    dep_end = face_kappa[:, -1, 96:128]
    own_right = lift[1] * face_kappa[:, :, 32:64, None]
    own_top = lift[3] * face_kappa[:, :, 96:128, None]
    sent_lat = from_behind(lift[0][None] * lat_end[:, :, None], "lat", 1)
    sent_dep = passed_along(lift[2][None] * dep_end[:, :, None], "dep", 1)
    left_tiles = jnp.concatenate(
        [sent_lat[None], lift[0] * face_kappa[:-1, :, 32:64, None]], axis=0
    )
    below_tiles = jnp.concatenate(
        [sent_dep[:, None], lift[2] * face_kappa[:, :-1, 96:128, None]], axis=1
    )
    couple = jnp.concatenate([left_tiles, own_right, below_tiles, own_top], axis=2)
    columns = rhs.shape[2]
    start_factor, inverse = factor(lax.psum(inner_local(rhs, rhs), ("lat", "dep")))
    basis_list = [combine_columns(rhs, inverse)]
    coef_table = []
    for step_index in range(KRY):
        image_block = apply_operator(basis_list[step_index], diag_tiles, couple, select)
        local_prods = jnp.stack(
            [inner_local(basis_list[prior], image_block) for prior in range(step_index + 1)]
        )
        coef_stack = lax.psum(local_prods, ("lat", "dep"))
        for prior in range(step_index + 1):
            image_block = image_block - combine_columns(basis_list[prior], coef_stack[prior])
        gram_matrix = lax.psum(inner_local(image_block, image_block), ("lat", "dep"))
        upper_factor, inverse = factor(gram_matrix)
        column_coefs = [coef_stack[prior] for prior in range(step_index + 1)]
        column_coefs.append(upper_factor)
        coef_table.append(column_coefs)
        basis_list.append(combine_columns(image_block, inverse))
    zero_small = jnp.zeros((columns, columns), jnp.float32)
    block_rows = []
    for row_index in range(KRY + 1):
        row_blocks = []
        for col_index in range(KRY):
            if row_index <= col_index + 1:
                row_blocks.append(coef_table[col_index][row_index])
            else:
                row_blocks.append(zero_small)
        block_rows.append(jnp.concatenate(row_blocks, axis=1))
    hessenberg = jnp.concatenate(block_rows, axis=0)
    gram_small = jnp.dot(hessenberg.T, hessenberg, precision=highest)
    right_side = jnp.dot(hessenberg[:columns].T, start_factor, precision=highest)
    coeffs = jax.scipy.linalg.cho_solve((jnp.linalg.cholesky(gram_small), True), right_side)
    update = combine_columns(basis_list[0], coeffs[:columns])
    for step_index in range(1, KRY):
        update = update + combine_columns(
            basis_list[step_index], coeffs[step_index * columns : (step_index + 1) * columns]
        )
    return update


def solution(mesh):
    in_specs = (
        P("lat", "dep", None),
        P("lat", "dep", None),
        P("lat", "dep"),
        P(),
        P(),
        P("lat", "dep", None, None),
    )
    out_specs = P("lat", "dep", None, None)
    return jax.shard_map(
        per_device, mesh=mesh, in_specs=in_specs, out_specs=out_specs, check_vma=False
    )
```

profile of v0, /device:TPU:1, one launch (start us, length us, event | category | flops | bytes accessed | tf_op | source)
XLA Modules:
  0.0 1614.5 jit_solution(5282608771596217027)
XLA Ops:
  1.6 68.8 %psum.119 = f32[32,32]{0,1:T(8,128)S(1)} all-reduce(f32[32,32]{0,1:T(8,128)S(1)} %convolution_bitcast_fusion.97), channel_id=1, replica_groups=mesh['lat'=16,'dep'=8] {'lat','dep'}, use_global_device_ids=true, to_apply=%region_0.1 | all-reduce | flops 1024 | bytes 8192 | tf_op jit(solution)/shard_map/psum | solution.py:141
  79.8 4.8 collective-permute-start.1
  91.2 50.8 %while.18 = (s32[]{:T(128)}, f32[4,8,128,128]{3,2,1,0:T(8,128)S(1)}, f32[4,8,128]{2,1,0:T(8,128)S(1)}, f32[3,64,64]{2,0,1:T(4,128)S(1)}, f32[4,8,128]{2,1,0:T(8,...) while((s32[]{:T(128)}, ...), condition=%wide.region_4.7_spmd.clone.clone, body=%wide.region_3.6_spmd.clone.clone.sunk | while | flops 63704832 | bytes 7220429 | solution.py:126
  172.6 65.2 %psum.120 = f32[32,32]{0,1:T(8,128)S(1)} all-reduce(f32[32,32]{0,1:T(8,128)} %convolution_bitcast_fusion.95), channel_id=1, replica_groups=mesh['lat'=16,'dep'=8] {'lat','dep'}, use_global_device_ids=true, to_apply=%region_5.8 | all-reduce | flops 1024 | bytes 8192 | tf_op jit(solution)/shard_map/psum | solution.py:149
  240.1 64.2 %psum.121 = f32[32,32]{0,1:T(8,128)S(1)} all-reduce(f32[32,32]{0,1:T(8,128)S(1)} %convolution_bitcast_fusion.94), channel_id=1, replica_groups=mesh['lat'=16,'dep'=8] {'lat','dep'}, use_global_device_ids=true, to_apply=%region_6.9 | all-reduce | flops 1024 | bytes 8192 | tf_op jit(solution)/shard_map/psum | solution.py:152
  322.7 4.8 collective-permute-start.7
  344.4 62.0 %psum.122 = f32[2,32,32]{1,2,0:T(8,128)S(1)} all-reduce(f32[2,32,32]{1,2,0:T(8,128)S(1)} %pad_maximum_fusion.5), channel_id=1, replica_groups=mesh['lat'=16,'dep'=8] {'lat','dep'}, use_global_device_ids=true, to_apply=%region_7.10 | all-reduce | flops 2048 | bytes 16384 | tf_op jit(solution)/shard_map/psum | solution.py:149
  410.1 63.5 %psum.123 = f32[32,32]{0,1:T(8,128)S(1)} all-reduce(f32[32,32]{0,1:T(8,128)S(1)} %convolution_bitcast_fusion.90), channel_id=1, replica_groups=mesh['lat'=16,'dep'=8] {'lat','dep'}, use_global_device_ids=true, to_apply=%region_8.11 | all-reduce | flops 1024 | bytes 8192 | tf_op jit(solution)/shard_map/psum | solution.py:152
  490.8 4.8 collective-permute-start.11
  507.8 4.3 convolution_subtract_fusion.5
  513.9 62.9 %psum.124 = f32[3,32,32]{1,2,0:T(8,128)S(1)} all-reduce(f32[3,32,32]{1,2,0:T(8,128)S(1)} %pad_maximum_fusion.4), channel_id=1, replica_groups=mesh['lat'=16,'dep'=8] {'lat','dep'}, use_global_device_ids=true, to_apply=%region_9.12 | all-reduce | flops 3072 | bytes 24576 | tf_op jit(solution)/shard_map/psum | solution.py:149
  581.1 64.3 %psum.125 = f32[32,32]{0,1:T(8,128)S(1)} all-reduce(f32[32,32]{0,1:T(8,128)S(1)} %convolution_bitcast_fusion.85), channel_id=1, replica_groups=mesh['lat'=16,'dep'=8] {'lat','dep'}, use_global_device_ids=true, to_apply=%region_10.13 | all-reduce | flops 1024 | bytes 8192 | tf_op jit(solution)/shard_map/psum | solution.py:152
  662.6 4.8 collective-permute-start.15
  685.9 63.0 %psum.126 = f32[4,32,32]{1,2,0:T(8,128)S(1)} all-reduce(f32[4,32,32]{1,2,0:T(8,128)S(1)} %pad_maximum_fusion.3), channel_id=1, replica_groups=mesh['lat'=16,'dep'=8] {'lat','dep'}, use_global_device_ids=true, to_apply=%region_11.14 | all-reduce | flops 4096 | bytes 32768 | tf_op jit(solution)/shard_map/psum | solution.py:149
  753.7 63.5 %psum.127 = f32[32,32]{0,1:T(8,128)S(1)} all-reduce(f32[32,32]{0,1:T(8,128)S(1)} %convolution_bitcast_fusion.79), channel_id=1, replica_groups=mesh['lat'=16,'dep'=8] {'lat','dep'}, use_global_device_ids=true, to_apply=%region_12.15 | all-reduce | flops 1024 | bytes 8192 | tf_op jit(solution)/shard_map/psum | solution.py:152
  836.5 4.8 collective-permute-start.19
  860.7 62.7 %psum.128 = f32[5,32,32]{1,2,0:T(8,128)S(1)} all-reduce(f32[5,32,32]{1,2,0:T(8,128)S(1)} %fusion.76), channel_id=1, replica_groups=mesh['lat'=16,'dep'=8] {'lat','dep'}, use_global_device_ids=true, to_apply=%region_13.16 | all-reduce | flops 5120 | bytes 40960 | tf_op jit(solution)/shard_map/psum | solution.py:149
  928.8 64.2 %psum.129 = f32[32,32]{0,1:T(8,128)S(1)} all-reduce(f32[32,32]{0,1:T(8,128)S(1)} %convolution_bitcast_fusion.72), channel_id=1, replica_groups=mesh['lat'=16,'dep'=8] {'lat','dep'}, use_global_device_ids=true, to_apply=%region_14.17 | all-reduce | flops 1024 | bytes 8192 | tf_op jit(solution)/shard_map/psum | solution.py:152
  1011.7 4.8 collective-permute-start.23
  1036.6 63.3 %psum.130 = f32[6,32,32]{1,2,0:T(8,128)S(1)} all-reduce(f32[6,32,32]{1,2,0:T(8,128)S(1)} %fusion.70), channel_id=1, replica_groups=mesh['lat'=16,'dep'=8] {'lat','dep'}, use_global_device_ids=true, to_apply=%region_15.18 | all-reduce | flops 6144 | bytes 49152 | tf_op jit(solution)/shard_map/psum | solution.py:149
  1106.0 63.8 %psum.131 = f32[32,32]{0,1:T(8,128)S(1)} all-reduce(f32[32,32]{0,1:T(8,128)S(1)} %convolution_bitcast_fusion.64), channel_id=1, replica_groups=mesh['lat'=16,'dep'=8] {'lat','dep'}, use_global_device_ids=true, to_apply=%region_16.19 | all-reduce | flops 1024 | bytes 8192 | tf_op jit(solution)/shard_map/psum | solution.py:152
  1189.3 4.8 collective-permute-start.27
  1214.6 63.2 %psum.132 = f32[7,32,32]{1,2,0:T(8,128)S(1)} all-reduce(f32[7,32,32]{1,2,0:T(8,128)S(1)} %fusion.63), channel_id=1, replica_groups=mesh['lat'=16,'dep'=8] {'lat','dep'}, use_global_device_ids=true, to_apply=%region_17.20 | all-reduce | flops 7168 | bytes 57344 | tf_op jit(solution)/shard_map/psum | solution.py:149
  1284.5 64.2 %psum.133 = f32[32,32]{0,1:T(8,128)S(1)} all-reduce(f32[32,32]{0,1:T(8,128)S(1)} %convolution_bitcast_fusion.55), channel_id=1, replica_groups=mesh['lat'=16,'dep'=8] {'lat','dep'}, use_global_device_ids=true, to_apply=%region_18.21 | all-reduce | flops 1024 | bytes 8192 | tf_op jit(solution)/shard_map/psum | solution.py:152
  1367.0 4.8 collective-permute-start.31
  1390.9 63.0 %psum.134 = f32[8,32,32]{1,2,0:T(8,128)S(1)} all-reduce(f32[8,32,32]{1,2,0:T(8,128)S(1)} %fusion.55), channel_id=1, replica_groups=mesh['lat'=16,'dep'=8] {'lat','dep'}, use_global_device_ids=true, to_apply=%region_19.22 | all-reduce | flops 8192 | bytes 65536 | tf_op jit(solution)/shard_map/psum | solution.py:149
  1459.3 63.7 %psum.135 = f32[32,32]{0,1:T(8,128)S(1)} all-reduce(f32[32,32]{0,1:T(8,128)S(1)} %convolution_bitcast_fusion.45), channel_id=1, replica_groups=mesh['lat'=16,'dep'=8] {'lat','dep'}, use_global_device_ids=true, to_apply=%region_20.23 | all-reduce | flops 1024 | bytes 8192 | tf_op jit(solution)/shard_map/psum | solution.py:152
  1536.6 11.7 cholesky.77
  1551.2 9.8 custom-call.23
  1563.2 11.7 cholesky.132
  1579.7 5.1 while.17
  1584.8 20.8 %custom-call.24 = f32[2,128,128]{1,2,0:T(8,128)S(1)} custom-call(f32[2,128,128]{2,1,0:T(8,128)} %get-tuple-element.122), custom_call_target="InvertDiagBlocksLowerTriangular" | custom-call | tf_op jit(solution)/shard_map/jit(_cho_solve)/triangular_solve | solution.py:171
  (677 shorter events, 427.5 us)
Async XLA Ops:
  79.1 84.4 %collective-permute-start = (f32[1,8,1024]{2,1,0:T(8,128)}, f32[1,8,1024]{2,1,0:T(8,128)}, u32[]{:S(2)}, u32[]{:S(2)}) collective-permute-start(f32[1,8,1024]{2,1,0:T(8,128)} %slice.619), channel_id=1, source_target_pairs={{0,8},{8,16},{16,24},{24,32},{32,40},{40,48},{48,56},{56,64},{64,7... | collective-permute-start | bytes 98312 | tf_op jit(solution)/shard_map/ppermute | solution.py:19
  79.8 85.2 %collective-permute-start.1 = (f32[1,8,1024]{2,1,0:T(8,128)}, f32[1,8,1024]{2,1,0:T(8,128)}, u32[]{:S(2)}, u32[]{:S(2)}) collective-permute-start(f32[1,8,1024]{2,1,0:T(8,128)} %slice.623), channel_id=1, source_target_pairs={{8,0},{16,8},{24,16},{32,24},{40,32},{48,40},{56,48},{64,56},{72,6... | collective-permute-start | bytes 98312 | tf_op jit(solution)/shard_map/ppermute | solution.py:21
  85.4 70.7 %collective-permute-start.2 = (f32[1,4,1024]{2,1,0:T(4,128)}, f32[1,4,1024]{2,1,0:T(4,128)S(1)}, u32[]{:S(2)}, u32[]{:S(2)}) collective-permute-start(f32[1,4,1024]{2,1,0:T(4,128)} %slice.625), channel_id=1, source_target_pairs={{0,1},{1,2},{2,3},{3,4},{4,5},{5,6},{6,7},{8,9},{9,10},{10,11},{11... | collective-permute-start | bytes 49160 | tf_op jit(solution)/shard_map/ppermute | solution.py:19
  89.1 73.0 %collective-permute-start.3 = (f32[1,4,1024]{2,1,0:T(4,128)}, f32[1,4,1024]{2,1,0:T(4,128)}, u32[]{:S(2)}, u32[]{:S(2)}) collective-permute-start(f32[1,4,1024]{2,1,0:T(4,128)} %slice.629), channel_id=1, source_target_pairs={{1,0},{2,1},{3,2},{4,3},{5,4},{6,5},{7,6},{9,8},{10,9},{11,10},{12... | collective-permute-start | bytes 49160 | tf_op jit(solution)/shard_map/ppermute | solution.py:21
  142.8 23.7 %collective-permute-start.4 = (f32[8,32,128]{2,1,0:T(8,128)}, f32[8,32,128]{2,1,0:T(8,128)}, u32[]{:S(2)}, u32[]{:S(2)}) collective-permute-start(f32[8,32,128]{2,1,0:T(8,128)} %broadcast_multiply_fusion.4), channel_id=1, source_target_pairs={{0,8},{8,16},{16,24},{24,32},{32,40},{40,48},{48,56},{56,64},{64,7... | collective-permute-start | bytes 393224 | tf_op jit(solution)/shard_map/ppermute | solution.py:31
  156.0 10.5 collective-permute-start.5
  321.9 15.0 collective-permute-start.6
  322.7 15.2 collective-permute-start.7
  327.5 5.6 collective-permute-start.8
  331.2 5.1 collective-permute-start.9
  490.7 16.1 collective-permute-start.10
  490.8 16.1 collective-permute-start.11
  496.6 8.8 collective-permute-start.12
  500.7 5.4 collective-permute-start.13
  662.5 15.7 collective-permute-start.14
  662.6 15.7 collective-permute-start.15
  668.4 8.4 collective-permute-start.16
  672.2 5.2 collective-permute-start.17
  835.8 15.8 collective-permute-start.18
  836.5 15.9 collective-permute-start.19
  842.2 7.7 collective-permute-start.20
  845.9 5.1 collective-permute-start.21
  1010.9 16.1 collective-permute-start.22
  1011.7 16.1 collective-permute-start.23
  1017.4 7.6 collective-permute-start.24
  1021.2 5.1 collective-permute-start.25
  1188.5 15.9 collective-permute-start.26
  1189.3 16.0 collective-permute-start.27
  1195.0 6.5 collective-permute-start.28
  1366.7 14.9 collective-permute-start.30
  1367.0 14.8 collective-permute-start.31
  1372.7 7.2 collective-permute-start.32
  (93 other events, 1334.6 us)
where the time goes:
time: 1630 us; the launch traced here: 1610 us
  blocking collectives  1090 us (67%)
  matrix products  178 us (11%)
  other arithmetic  138 us (8%)
  local copies, waits for them, and re-layouts  118 us (7%)
  starting transfers between devices  83.3 us (5%)
    psum x8, blocking collectives, per_device(): lax.psum(inner_local(image_block, image_block), ('lat', 'dep'))  511 us
    psum x8, blocking collectives, per_device(): coef_stack = lax.psum(local_prods, ('lat', 'dep'))  505 us
    psum x1, blocking collectives, per_device(): lax.psum(inner_local(rhs, rhs), ('lat', 'dep'))  68.8 us
    ppermute x16, starting transfers between devices, with_halo(): lax.ppermute(head, axis, [((i + 1) % count, i) for i in range(ends)])  54.5 us
    dot_general x52, matrix products, combine_columns(): return jnp.einsum('aevu,vw->aewu', vectors, matrix, precision=highest)  46.2 us
    another operation x7, other arithmetic, per_device(): jnp.linalg.cholesky(gram_small)  35.7 us
    dot_general x8, matrix products, apply_operator(): jnp.einsum('aeki,aevk->aevi', couple, near_traces, precision=highest)  34.6 us
    dot_general x8, matrix products, apply_operator(): jnp.einsum('aeij,aevj->aevi', diag_tiles, vectors, precision=highest)  33.2 us
  transfers between devices with their start and end apart: 34, of which 5 were waited for; matrix products, arithmetic and copies ran while one was open for 7% of the time, Pallas kernels for 0%

commit v1 on v0

--- a/solution.py
+++ b/solution.py
@@ -146,7 +146,7 @@
         local_prods = jnp.stack(
             [inner_local(basis_list[prior], image_block) for prior in range(step_index + 1)]
         )
-        coef_stack = lax.psum(local_prods, ("lat", "dep"))
+        coef_stack = lax.psum(lax.psum(local_prods, "lat"), "dep")
         for prior in range(step_index + 1):
             image_block = image_block - combine_columns(basis_list[prior], coef_stack[prior])
         gram_matrix = lax.psum(inner_local(image_block, image_block), ("lat", "dep"))

time: 1630 us -> 1850 us (1.13)
  blocking collectives: 1090 us -> 1320 us
    psum x8 -> x16, blocking collectives: 505 us -> 728 us  [per_device(): coef_stack = lax.psum(lax.psum(local_prods, 'lat'), 'dep')]
  transfers between devices with their start and end apart: 34 -> 34, of which waited for: 5 -> 3; matrix products, arithmetic and copies ran while one was open for 7% -> 6% of each run, Pallas kernels for 0% -> 0%
where the time goes in v1:
time: 1850 us; the launch traced here: 1840 us
  blocking collectives  1320 us (71%)
  matrix products  177 us (10%)
  other arithmetic  138 us (7%)
  local copies, waits for them, and re-layouts  118 us (6%)
  starting transfers between devices  82.4 us (4%)
    psum x16, blocking collectives, per_device(): coef_stack = lax.psum(lax.psum(local_prods, 'lat'), 'dep')  728 us
    psum x8, blocking collectives, per_device(): lax.psum(inner_local(image_block, image_block), ('lat', 'dep'))  519 us
    psum x1, blocking collectives, per_device(): lax.psum(inner_local(rhs, rhs), ('lat', 'dep'))  68.8 us
    ppermute x16, starting transfers between devices, with_halo(): lax.ppermute(head, axis, [((i + 1) % count, i) for i in range(ends)])  61.7 us
    dot_general x52, matrix products, combine_columns(): return jnp.einsum('aevu,vw->aewu', vectors, matrix, precision=highest)  46.2 us
  transfers between devices with their start and end apart: 34, of which 3 were waited for; matrix products, arithmetic and copies ran while one was open for 6% of the time, Pallas kernels for 0%

profile of v1, /device:TPU:1, one launch (start us, length us, event | category | flops | bytes accessed | tf_op | source)
XLA Modules:
  0.0 1839.0 jit_solution(5068652634615666579)
XLA Ops:
  1.6 68.8 %psum.175 = f32[32,32]{0,1:T(8,128)S(1)} all-reduce(f32[32,32]{0,1:T(8,128)S(1)} %convolution_bitcast_fusion.97), channel_id=1, replica_groups=mesh['lat'=16,'dep'=8] {'lat','dep'}, use_global_device_ids=true, to_apply=%region_0.1 | all-reduce | flops 1024 | bytes 8192 | tf_op jit(solution)/shard_map/psum | solution.py:141
  91.4 50.7 %while.18 = (s32[]{:T(128)}, f32[4,8,128,128]{3,2,1,0:T(8,128)S(1)}, f32[4,8,128]{2,1,0:T(8,128)S(1)}, f32[3,64,64]{2,0,1:T(4,128)S(1)}, f32[4,8,128]{2,1,0:T(8,...) while((s32[]{:T(128)}, ...), condition=%wide.region_4.7_spmd.clone.clone, body=%wide.region_3.6_spmd.clone.clone.sunk | while | flops 63704832 | bytes 7220429 | solution.py:126
  172.2 60.8 %psum.176 = f32[1,32,32]{1,2,0:T(8,128)S(1)} all-reduce(f32[1,32,32]{1,2,0:T(8,128)S(1)} %convolution_bitcast_fusion.95), channel_id=1, replica_groups=mesh['lat'=16,'dep'=8] {'lat'}, use_global_device_ids=true, to_apply=%region_5.8 | all-reduce | flops 1024 | bytes 8192 | tf_op jit(solution)/shard_map/psum | solution.py:149
  233.0 32.4 %psum.177 = f32[32,32]{0,1:T(8,128)S(1)} all-reduce(f32[32,32]{0,1:T(8,128)S(1)} %bitcast.1183), channel_id=1, replica_groups=mesh['lat'=16,'dep'=8] {'dep'}, use_global_device_ids=true, to_apply=%region_6.9 | all-reduce | flops 1024 | bytes 8192 | tf_op jit(solution)/shard_map/psum | solution.py:149
  267.6 65.3 %psum.178 = f32[32,32]{0,1:T(8,128)S(1)} all-reduce(f32[32,32]{0,1:T(8,128)S(1)} %convolution_bitcast_fusion.94), channel_id=1, replica_groups=mesh['lat'=16,'dep'=8] {'lat','dep'}, use_global_device_ids=true, to_apply=%region_7.10 | all-reduce | flops 1024 | bytes 8192 | tf_op jit(solution)/shard_map/psum | solution.py:152
  371.3 56.0 %psum.179 = f32[2,32,32]{1,2,0:T(8,128)S(1)} all-reduce(f32[2,32,32]{1,2,0:T(8,128)S(1)} %pad_maximum_fusion.5), channel_id=1, replica_groups=mesh['lat'=16,'dep'=8] {'lat'}, use_global_device_ids=true, to_apply=%region_8.11 | all-reduce | flops 2048 | bytes 16384 | tf_op jit(solution)/shard_map/psum | solution.py:149
  427.3 34.1 %psum.180 = f32[2,32,32]{1,2,0:T(8,128)S(1)} all-reduce(f32[2,32,32]{1,2,0:T(8,128)S(1)} %psum.179), channel_id=1, replica_groups=mesh['lat'=16,'dep'=8] {'dep'}, use_global_device_ids=true, to_apply=%region_9.12 | all-reduce | flops 2048 | bytes 16384 | tf_op jit(solution)/shard_map/psum | solution.py:149
  465.0 65.0 %psum.181 = f32[32,32]{0,1:T(8,128)S(1)} all-reduce(f32[32,32]{0,1:T(8,128)S(1)} %convolution_bitcast_fusion.90), channel_id=1, replica_groups=mesh['lat'=16,'dep'=8] {'lat','dep'}, use_global_device_ids=true, to_apply=%region_10.13 | all-reduce | flops 1024 | bytes 8192 | tf_op jit(solution)/shard_map/psum | solution.py:152
  547.2 4.8 collective-permute-start.11
  570.3 55.7 %psum.182 = f32[3,32,32]{1,2,0:T(8,128)S(1)} all-reduce(f32[3,32,32]{1,2,0:T(8,128)S(1)} %pad_maximum_fusion.4), channel_id=1, replica_groups=mesh['lat'=16,'dep'=8] {'lat'}, use_global_device_ids=true, to_apply=%region_11.14 | all-reduce | flops 3072 | bytes 24576 | tf_op jit(solution)/shard_map/psum | solution.py:149
  626.1 34.1 %psum.183 = f32[3,32,32]{1,2,0:T(8,128)S(1)} all-reduce(f32[3,32,32]{1,2,0:T(8,128)S(1)} %psum.182), channel_id=1, replica_groups=mesh['lat'=16,'dep'=8] {'dep'}, use_global_device_ids=true, to_apply=%region_12.15 | all-reduce | flops 3072 | bytes 24576 | tf_op jit(solution)/shard_map/psum | solution.py:149
  664.4 64.9 %psum.184 = f32[32,32]{0,1:T(8,128)S(1)} all-reduce(f32[32,32]{0,1:T(8,128)S(1)} %convolution_bitcast_fusion.85), channel_id=1, replica_groups=mesh['lat'=16,'dep'=8] {'lat','dep'}, use_global_device_ids=true, to_apply=%region_13.16 | all-reduce | flops 1024 | bytes 8192 | tf_op jit(solution)/shard_map/psum | solution.py:152
  769.6 55.7 %psum.185 = f32[4,32,32]{1,2,0:T(8,128)S(1)} all-reduce(f32[4,32,32]{1,2,0:T(8,128)S(1)} %pad_maximum_fusion.3), channel_id=1, replica_groups=mesh['lat'=16,'dep'=8] {'lat'}, use_global_device_ids=true, to_apply=%region_14.17 | all-reduce | flops 4096 | bytes 32768 | tf_op jit(solution)/shard_map/psum | solution.py:149
  825.3 34.4 %psum.186 = f32[4,32,32]{1,2,0:T(8,128)S(1)} all-reduce(f32[4,32,32]{1,2,0:T(8,128)S(1)} %psum.185), channel_id=1, replica_groups=mesh['lat'=16,'dep'=8] {'dep'}, use_global_device_ids=true, to_apply=%region_15.18 | all-reduce | flops 4096 | bytes 32768 | tf_op jit(solution)/shard_map/psum | solution.py:149
  864.5 64.7 %psum.187 = f32[32,32]{0,1:T(8,128)S(1)} all-reduce(f32[32,32]{0,1:T(8,128)S(1)} %convolution_bitcast_fusion.79), channel_id=1, replica_groups=mesh['lat'=16,'dep'=8] {'lat','dep'}, use_global_device_ids=true, to_apply=%region_16.19 | all-reduce | flops 1024 | bytes 8192 | tf_op jit(solution)/shard_map/psum | solution.py:152
  971.8 56.4 %psum.188 = f32[5,32,32]{1,2,0:T(8,128)S(1)} all-reduce(f32[5,32,32]{1,2,0:T(8,128)S(1)} %fusion.76), channel_id=1, replica_groups=mesh['lat'=16,'dep'=8] {'lat'}, use_global_device_ids=true, to_apply=%region_17.20 | all-reduce | flops 5120 | bytes 40960 | tf_op jit(solution)/shard_map/psum | solution.py:149
  1028.2 34.6 %psum.189 = f32[5,32,32]{1,2,0:T(8,128)S(1)} all-reduce(f32[5,32,32]{1,2,0:T(8,128)S(1)} %psum.188), channel_id=1, replica_groups=mesh['lat'=16,'dep'=8] {'dep'}, use_global_device_ids=true, to_apply=%region_18.21 | all-reduce | flops 5120 | bytes 40960 | tf_op jit(solution)/shard_map/psum | solution.py:149
  1068.2 64.8 %psum.190 = f32[32,32]{0,1:T(8,128)S(1)} all-reduce(f32[32,32]{0,1:T(8,128)S(1)} %convolution_bitcast_fusion.72), channel_id=1, replica_groups=mesh['lat'=16,'dep'=8] {'lat','dep'}, use_global_device_ids=true, to_apply=%region_19.22 | all-reduce | flops 1024 | bytes 8192 | tf_op jit(solution)/shard_map/psum | solution.py:152
  1176.2 56.8 %psum.191 = f32[6,32,32]{1,2,0:T(8,128)S(1)} all-reduce(f32[6,32,32]{1,2,0:T(8,128)S(1)} %fusion.70), channel_id=1, replica_groups=mesh['lat'=16,'dep'=8] {'lat'}, use_global_device_ids=true, to_apply=%region_20.23 | all-reduce | flops 6144 | bytes 49152 | tf_op jit(solution)/shard_map/psum | solution.py:149
  1233.0 34.5 %psum.192 = f32[6,32,32]{1,2,0:T(8,128)S(1)} all-reduce(f32[6,32,32]{1,2,0:T(8,128)S(1)} %psum.191), channel_id=1, replica_groups=mesh['lat'=16,'dep'=8] {'dep'}, use_global_device_ids=true, to_apply=%region_21.24 | all-reduce | flops 6144 | bytes 49152 | tf_op jit(solution)/shard_map/psum | solution.py:149
  1273.6 64.7 %psum.193 = f32[32,32]{0,1:T(8,128)S(1)} all-reduce(f32[32,32]{0,1:T(8,128)S(1)} %convolution_bitcast_fusion.64), channel_id=1, replica_groups=mesh['lat'=16,'dep'=8] {'lat','dep'}, use_global_device_ids=true, to_apply=%region_22.25 | all-reduce | flops 1024 | bytes 8192 | tf_op jit(solution)/shard_map/psum | solution.py:152
  1382.3 56.9 %psum.194 = f32[7,32,32]{1,2,0:T(8,128)S(1)} all-reduce(f32[7,32,32]{1,2,0:T(8,128)S(1)} %fusion.63), channel_id=1, replica_groups=mesh['lat'=16,'dep'=8] {'lat'}, use_global_device_ids=true, to_apply=%region_23.26 | all-reduce | flops 7168 | bytes 57344 | tf_op jit(solution)/shard_map/psum | solution.py:149
  1439.2 34.0 %psum.195 = f32[7,32,32]{1,2,0:T(8,128)S(1)} all-reduce(f32[7,32,32]{1,2,0:T(8,128)S(1)} %psum.194), channel_id=1, replica_groups=mesh['lat'=16,'dep'=8] {'dep'}, use_global_device_ids=true, to_apply=%region_24.27 | all-reduce | flops 7168 | bytes 57344 | tf_op jit(solution)/shard_map/psum | solution.py:149
  1480.0 64.6 %psum.196 = f32[32,32]{0,1:T(8,128)S(1)} all-reduce(f32[32,32]{0,1:T(8,128)S(1)} %convolution_bitcast_fusion.55), channel_id=1, replica_groups=mesh['lat'=16,'dep'=8] {'lat','dep'}, use_global_device_ids=true, to_apply=%region_25.28 | all-reduce | flops 1024 | bytes 8192 | tf_op jit(solution)/shard_map/psum | solution.py:152
  1586.0 56.7 %psum.197 = f32[8,32,32]{1,2,0:T(8,128)S(1)} all-reduce(f32[8,32,32]{1,2,0:T(8,128)S(1)} %fusion.55), channel_id=1, replica_groups=mesh['lat'=16,'dep'=8] {'lat'}, use_global_device_ids=true, to_apply=%region_26.29 | all-reduce | flops 8192 | bytes 65536 | tf_op jit(solution)/shard_map/psum | solution.py:149
  1642.8 34.8 %psum.198 = f32[8,32,32]{1,2,0:T(8,128)S(1)} all-reduce(f32[8,32,32]{1,2,0:T(8,128)S(1)} %psum.197), channel_id=1, replica_groups=mesh['lat'=16,'dep'=8] {'dep'}, use_global_device_ids=true, to_apply=%region_27.30 | all-reduce | flops 8192 | bytes 65536 | tf_op jit(solution)/shard_map/psum | solution.py:149
  1683.0 64.7 %psum.199 = f32[32,32]{0,1:T(8,128)S(1)} all-reduce(f32[32,32]{0,1:T(8,128)S(1)} %convolution_bitcast_fusion.45), channel_id=1, replica_groups=mesh['lat'=16,'dep'=8] {'lat','dep'}, use_global_device_ids=true, to_apply=%region_28.31 | all-reduce | flops 1024 | bytes 8192 | tf_op jit(solution)/shard_map/psum | solution.py:152
  1761.3 11.7 cholesky.77
  1776.0 9.8 custom-call.23
  1788.0 11.7 cholesky.132
  1804.6 5.0 while.17
  1809.6 20.7 %custom-call.24 = f32[2,128,128]{1,2,0:T(8,128)S(1)} custom-call(f32[2,128,128]{2,1,0:T(8,128)} %get-tuple-element.122), custom_call_target="InvertDiagBlocksLowerTriangular" | custom-call | tf_op jit(solution)/shard_map/jit(_cho_solve)/triangular_solve | solution.py:171
  (685 shorter events, 460.3 us)
Async XLA Ops:
  79.3 84.3 %collective-permute-start = (f32[1,8,1024]{2,1,0:T(8,128)}, f32[1,8,1024]{2,1,0:T(8,128)}, u32[]{:S(2)}, u32[]{:S(2)}) collective-permute-start(f32[1,8,1024]{2,1,0:T(8,128)} %slice.619), channel_id=1, source_target_pairs={{0,8},{8,16},{16,24},{24,32},{32,40},{40,48},{48,56},{56,64},{64,7... | collective-permute-start | bytes 98312 | tf_op jit(solution)/shard_map/ppermute | solution.py:19
  80.0 85.1 %collective-permute-start.1 = (f32[1,8,1024]{2,1,0:T(8,128)}, f32[1,8,1024]{2,1,0:T(8,128)}, u32[]{:S(2)}, u32[]{:S(2)}) collective-permute-start(f32[1,8,1024]{2,1,0:T(8,128)} %slice.623), channel_id=1, source_target_pairs={{8,0},{16,8},{24,16},{32,24},{40,32},{48,40},{56,48},{64,56},{72,6... | collective-permute-start | bytes 98312 | tf_op jit(solution)/shard_map/ppermute | solution.py:21
  85.6 70.6 %collective-permute-start.2 = (f32[1,4,1024]{2,1,0:T(4,128)}, f32[1,4,1024]{2,1,0:T(4,128)S(1)}, u32[]{:S(2)}, u32[]{:S(2)}) collective-permute-start(f32[1,4,1024]{2,1,0:T(4,128)} %slice.625), channel_id=1, source_target_pairs={{0,1},{1,2},{2,3},{3,4},{4,5},{5,6},{6,7},{8,9},{9,10},{10,11},{11... | collective-permute-start | bytes 49160 | tf_op jit(solution)/shard_map/ppermute | solution.py:19
  89.3 72.8 %collective-permute-start.3 = (f32[1,4,1024]{2,1,0:T(4,128)}, f32[1,4,1024]{2,1,0:T(4,128)}, u32[]{:S(2)}, u32[]{:S(2)}) collective-permute-start(f32[1,4,1024]{2,1,0:T(4,128)} %slice.629), channel_id=1, source_target_pairs={{1,0},{2,1},{3,2},{4,3},{5,4},{6,5},{7,6},{9,8},{10,9},{11,10},{12... | collective-permute-start | bytes 49160 | tf_op jit(solution)/shard_map/ppermute | solution.py:21
  143.1 23.6 %collective-permute-start.4 = (f32[8,32,128]{2,1,0:T(8,128)}, f32[8,32,128]{2,1,0:T(8,128)}, u32[]{:S(2)}, u32[]{:S(2)}) collective-permute-start(f32[8,32,128]{2,1,0:T(8,128)} %broadcast_multiply_fusion.4), channel_id=1, source_target_pairs={{0,8},{8,16},{16,24},{24,32},{32,40},{40,48},{48,56},{56,64},{64,7... | collective-permute-start | bytes 393224 | tf_op jit(solution)/shard_map/ppermute | solution.py:31
  156.2 10.5 collective-permute-start.5
  350.4 13.4 collective-permute-start.6
  351.2 13.6 collective-permute-start.7
  358.1 5.1 collective-permute-start.9
  547.1 16.1 collective-permute-start.10
  547.2 16.1 collective-permute-start.11
  553.0 8.8 collective-permute-start.12
  555.9 6.6 collective-permute-start.13
  746.3 15.6 collective-permute-start.14
  746.4 15.6 collective-permute-start.15
  752.2 8.3 collective-permute-start.16
  755.0 6.1 collective-permute-start.17
  947.7 15.1 collective-permute-start.18
  948.4 15.2 collective-permute-start.19
  954.2 7.2 collective-permute-start.20
  956.2 5.9 collective-permute-start.21
  1151.0 15.6 collective-permute-start.22
  1151.8 15.6 collective-permute-start.23
  1157.5 7.6 collective-permute-start.24
  1160.4 5.4 collective-permute-start.25
  1356.9 15.2 collective-permute-start.26
  1357.7 15.2 collective-permute-start.27
  1363.4 6.6 collective-permute-start.28
  1366.3 5.1 collective-permute-start.29
  1562.8 14.0 collective-permute-start.30
  1562.9 13.9 collective-permute-start.31
  1568.7 7.4 collective-permute-start.32
  (93 other events, 1433.8 us)
